TPU v7x, 256 devices: a whole 4x4x8 slice. The times are simulated.
256 devices in a mesh: vox: 64 (over y, z, core), comp: 4 (over x).
Axes of the slice: x: 4, y: 4, z: 8, core: 2. Of those that a mesh axis runs over, the one named last changes fastest.
Arguments:
- data: bfloat16 [2048, 65536], P('comp', 'vox'), may hold values from -108 to 108
- projection: bfloat16 [512, 2048], P(None, 'comp'), may hold values from -0.125 to 0.125
- initial: float32 [512, 512], P('comp'), may hold values from -0.25 to 0.25
Outputs:
- unmixing: float32 [512, 512], P('comp')
- sources: bfloat16 [512, 65536], P('comp', 'vox')
All inputs are finite; a program needn't handle non-finite values.
Results may differ from a plain program's by a relative error of at most 0.008.
Values may be sent and summed in bfloat16 or wider, within the bound.
A program may use at most 64 MiB of HBM per device.

v0:
```python
import jax
import jax.numpy as jnp
from jax import lax
from jax.sharding import PartitionSpec as P

ICA_ITERS = 2
WHITEN_STEPS = 3
DECOR_STEPS = 3


def mult(left, right):
    return jnp.dot(left, right, precision=lax.Precision.HIGHEST)


def inner(left, right):
    return lax.dot_general(
        left, right, (((1,), (1,)), ((), ())), preferred_element_type=jnp.float32
    )


def whitening(covar):
    count = covar.shape[0]
    eye = jnp.eye(count, dtype=jnp.float32)
    cscale = jnp.sqrt(jnp.sum(covar * covar) + 1e-06)
    ymat = covar / cscale
    zmat = eye
    for step in range(WHITEN_STEPS):
        middle = 1.5 * eye - 0.5 * mult(zmat, ymat)
        ymat = mult(ymat, middle)
        zmat = mult(middle, zmat)
    return (zmat / jnp.sqrt(cscale)).astype(jnp.bfloat16)


def decorrelate(newer):
    gram = mult(newer, newer.T)
    newer = newer / jnp.sqrt(jnp.sqrt(jnp.sum(gram * gram) + 1e-06))
    for step in range(DECOR_STEPS):
        newer = 1.5 * newer - 0.5 * mult(mult(newer, newer.T), newer)
    return newer


def shards(data, projection, initial):
    rows_here = initial.shape[0]
    voxels = data.shape[1] * lax.axis_size("vox")
    start_row = lax.axis_index("comp") * rows_here
    reduced_rows = lax.psum_scatter(
        jnp.dot(projection, data, preferred_element_type=jnp.float32),
        "comp",
        scatter_dimension=0,
        tiled=True,
    ).astype(jnp.bfloat16)
    reduced = lax.all_gather(reduced_rows, "comp", axis=0, tiled=True)
    cov_part = inner(reduced_rows, reduced)
    cov_summed = lax.psum(cov_part, "vox")
    covar = lax.all_gather(cov_summed, "comp", axis=0, tiled=True)
    covar = covar / voxels
    whiten = whitening(covar)
    whitened = jnp.dot(whiten, reduced, preferred_element_type=jnp.float32).astype(jnp.bfloat16)
    weights = initial
    for turn in range(ICA_ITERS):
        scores = jnp.dot(weights.astype(jnp.bfloat16), whitened, preferred_element_type=jnp.float32)
        bent = jnp.tanh(scores)
        pulled = inner(bent.astype(jnp.bfloat16), whitened)
        slope = jnp.sum(1.0 - bent * bent, axis=1)
        pulled, slope = lax.psum((pulled, slope), "vox")
        newer = pulled - slope[:, None] * weights
        whole = lax.all_gather(newer, "comp", axis=0, tiled=True)
        whole = decorrelate(whole)
        weights = lax.dynamic_slice_in_dim(whole, start_row, rows_here, 0)
    sources = jnp.dot(
        weights.astype(jnp.bfloat16), whitened, preferred_element_type=jnp.float32
    ).astype(jnp.bfloat16)
    return (weights, sources)


def solution(mesh):
    return jax.shard_map(
        shards,
        mesh=mesh,
        in_specs=(P("comp", "vox"), P(None, "comp"), P("comp", None)),
        out_specs=(P("comp", None), P("comp", "vox")),
        check_vma=False,
    )
```

profile of v0, /device:TPU:8, one launch (start us, length us, event | category | flops | bytes accessed | tf_op | source)
XLA Modules:
  0.0 767.6 jit_solution(10863912530842845717)
XLA Ops:
  8.4 3.1 fusion.26
  11.6 35.2 %reduce-scatter.2.cloned.1.call-done = f32[128,1024]{1,0:T(8,128)} async-done(((f32[512,1024]{1,0:T(8,128)}), f32[128,1024]{1,0:T(8,128)}) %reduce-scatter.2.cloned.1.call-update) | async-done | bytes 524304 | tf_op jit(solution)/shard_map/reduce_scatter | solution.py:46
  48.6 27.0 %all-gather.5.cloned.1.call-done = bf16[512,1024]{1,0:T(8,128)(2,1)} async-done(((bf16[128,1024]{1,0:T(8,128)(2,1)}), bf16[512,1024]{1,0:T(8,128)(2,1)}) %all-gather.5.cloned.1.call-update) | async-done | bytes 1048592 | tf_op jit(solution)/shard_map/all_gather | solution.py:52
  75.6 2.5 fusion.27
  78.2 178.1 %all-reduce.4.cloned.1.call-done = f32[128,512]{1,0:T(8,128)} async-done(((f32[128,512]{1,0:T(8,128)}), f32[128,512]{1,0:T(8,128)}) %all-reduce.4.cloned.1.call-update) | async-done | bytes 262160 | tf_op jit(solution)/shard_map/psum | solution.py:54
  256.3 26.8 %all-gather.7.cloned.1.call-done = f32[512,512]{1,0:T(8,128)} async-done(((f32[128,512]{1,0:T(8,128)}), f32[512,512]{1,0:T(8,128)}) %all-gather.7.cloned.1.call-update) | async-done | bytes 1048592 | tf_op jit(solution)/shard_map/all_gather | solution.py:55
  283.1 2.1 multiply_reduce_fusion
  285.9 2.3 select_subtract_fusion.2
  289.5 1.9 fusion.10
  291.4 1.9 select_subtract_fusion.1
  297.0 1.8 select_subtract_fusion
  298.9 13.2 %fusion.4 = bf16[512,512]{1,0:T(8,128)(2,1)S(1)} fusion(f32[512,512]{1,0:T(8,128)S(1)} %select_subtract_fusion, f32[512,512]{1,0:T(8,128)S(1)} %fusion.28, f32[]{:T(128)S(6)} %sqrt.19), kind=kOutput, calls=%fused_computation.18 | convolution fusion | flops 1611137024 | bytes 2621444 | tf_op jit(solution)/shard_map/dot_general | solution.py:12
  314.8 105.3 %psum.37 = f32[128]{0:T(128)S(1)} all-reduce(f32[128]{0:T(128)S(1)} %get-tuple-element.2), channel_id=1, replica_groups=mesh['vox'=64,'comp'=4] {'vox'}, use_global_device_ids=true, to_apply=%region_5.0 | all-reduce | flops 128 | bytes 1024 | tf_op jit(solution)/shard_map/psum | solution.py:65
  420.2 71.3 %all-reduce.6.cloned.1.call-done = f32[128,512]{1,0:T(8,128)} async-done(((f32[128,512]{1,0:T(8,128)}), f32[128,512]{1,0:T(8,128)}) %all-reduce.6.cloned.1.call-update) | async-done | bytes 262160 | tf_op jit(solution)/shard_map/psum | solution.py:65
  493.3 25.6 %all-gather.9.cloned.1.call-done = f32[512,512]{1,0:T(8,128)} async-done(((f32[128,512]{1,0:T(8,128)}), f32[512,512]{1,0:T(8,128)}) %all-gather.9.cloned.1.call-update) | async-done | bytes 1048592 | tf_op jit(solution)/shard_map/all_gather | solution.py:67
  519.0 4.2 fusion.6
  523.9 1.9 fusion.8
  525.8 1.9 fusion.3
  527.8 1.9 fusion.30
  529.6 1.9 fusion.2
  531.5 1.9 fusion.31
  533.4 2.8 fusion.32
  538.8 105.5 %psum.39 = f32[128]{0:T(128)S(1)} all-reduce(f32[128]{0:T(128)S(1)} %get-tuple-element.4), channel_id=1, replica_groups=mesh['vox'=64,'comp'=4] {'vox'}, use_global_device_ids=true, to_apply=%region_9.0 | all-reduce | flops 128 | bytes 1024 | tf_op jit(solution)/shard_map/psum | solution.py:65
  644.3 71.2 %all-reduce.8.cloned.1.call-done = f32[128,512]{1,0:T(8,128)} async-done(((f32[128,512]{1,0:T(8,128)}), f32[128,512]{1,0:T(8,128)}) %all-reduce.8.cloned.1.call-update) | async-done | bytes 262160 | tf_op jit(solution)/shard_map/psum | solution.py:65
  717.3 25.7 %all-gather.11.cloned.1.call-done = f32[512,512]{1,0:T(8,128)} async-done(((f32[128,512]{1,0:T(8,128)}), f32[512,512]{1,0:T(8,128)}) %all-gather.11.cloned.1.call-update) | async-done | bytes 1048592 | tf_op jit(solution)/shard_map/all_gather | solution.py:67
  743.1 4.2 fusion.7
  748.1 1.9 fusion.9
  750.0 1.9 fusion.1
  751.9 1.9 fusion.33
  753.7 1.9 fusion
  755.6 1.9 fusion.34
  757.5 1.8 fusion.35
  (45 shorter events, 18.1 us)
Async XLA Ops:
  7.2 1.2 copy-start
  7.2 39.6 %reduce-scatter.2.cloned.1.call-start = ((), (), s32[]{:S(2)}) async-start(), calls=%async_computation.1 | async-start | bytes 2621440 | tf_op jit(solution)/shard_map/reduce_scatter | solution.py:46
  11.5 64.1 %all-gather.5.cloned.1.call-start = ((), (), s32[]{:S(2)}) async-start(), calls=%async_computation.2 | async-start | bytes 1310720 | tf_op jit(solution)/shard_map/all_gather | solution.py:52
  48.6 207.7 %all-reduce.4.cloned.1.call-start = ((), (), s32[]{:S(2)}) async-start(), calls=%async_computation.3 | async-start | bytes 524288 | tf_op jit(solution)/shard_map/psum | solution.py:54
  78.1 205.0 %all-gather.7.cloned.1.call-start = ((), (), s32[]{:S(2)}) async-start(), calls=%async_computation.4 | async-start | bytes 1310720 | tf_op jit(solution)/shard_map/all_gather | solution.py:55
  256.3 235.2 %all-reduce.6.cloned.1.call-start = ((), (), s32[]{:S(2)}) async-start(), calls=%async_computation.5 | async-start | bytes 524288 | tf_op jit(solution)/shard_map/psum | solution.py:65
  288.3 1.2 copy-start.5
  298.9 13.2 %copy-start.4 = (bf16[512,1024]{1,0:T(8,128)(2,1)S(1)}, bf16[512,1024]{1,0:T(8,128)(2,1)}, u32[]{:S(2)}) copy-start(bf16[512,1024]{1,0:T(8,128)(2,1)} %all-gather.5.cloned.1.call-done) | copy-start | bytes 3145732
  312.1 1.0 copy-start.7
  314.8 204.2 %all-gather.9.cloned.1.call-start = ((), (), s32[]{:S(2)}) async-start(), calls=%async_computation.6 | async-start | bytes 1310720 | tf_op jit(solution)/shard_map/all_gather | solution.py:67
  493.3 222.2 %all-reduce.8.cloned.1.call-start = ((), (), s32[]{:S(2)}) async-start(), calls=%async_computation.7 | async-start | bytes 524288 | tf_op jit(solution)/shard_map/psum | solution.py:65
  519.0 5.0 copy-start.1
  538.8 204.3 %all-gather.11.cloned.1.call-start = ((), (), s32[]{:S(2)}) async-start(), calls=%async_computation.8 | async-start | bytes 1310720 | tf_op jit(solution)/shard_map/all_gather | solution.py:67
  743.1 5.0 copy-start.2
  748.0 1.9 copy-start.3
  759.4 1.0 copy-start.6
Sparse Core Ops, SparseCore 0:
  11.6 35.1 reduce-scatter.1
  49.2 26.3 all-gather.4
  79.7 176.5 all-reduce.3
  257.9 25.1 all-gather.6
  314.9 176.5 all-reduce.5
  493.8 25.1 all-gather.8
  538.9 176.5 all-reduce.7
  717.9 25.1 all-gather.10
where the time goes:
time: 777 us; the launch traced here: 768 us
  waiting for transfers between devices  461 us (59%)
  blocking collectives  211 us (27%)
  matrix products  69.2 us (9%)
  between operations  17 us (2%)
    psum x2, blocking collectives, shards(): pulled, slope = lax.psum((pulled, slope), 'vox')  211 us
    psum x1, waiting for transfers between devices, shards(): cov_summed = lax.psum(cov_part, 'vox')  178 us
    psum x2, waiting for transfers between devices, shards(): pulled, slope = lax.psum((pulled, slope), 'vox')  143 us
    dot_general x22, matrix products, mult(): return jnp.dot(left, right, precision=lax.Precision.HIGHEST)  57.7 us
    all_gather x2, waiting for transfers between devices, shards(): whole = lax.all_gather(newer, 'comp', axis=0, tiled=True)  51.4 us
    reduce_scatter x1, waiting for transfers between devices, shards(): lax.psum_scatter(jnp.dot(projection, data, preferred_element_type=jnp.flo...  35.2 us
    all_gather x1, waiting for transfers between devices, shards(): reduced = lax.all_gather(reduced_rows, 'comp', axis=0, tiled=True)  27 us
    all_gather x1, waiting for transfers between devices, shards(): covar = lax.all_gather(cov_summed, 'comp', axis=0, tiled=True)  26.8 us
  transfers between devices with their start and end apart: 8, of which 8 were waited for; matrix products, arithmetic and copies ran while one was open for 0% of the time, Pallas kernels for 0%

commit v1 on v0

--- a/solution.py
+++ b/solution.py
@@ -51,7 +51,7 @@
     ).astype(jnp.bfloat16)
     reduced = lax.all_gather(reduced_rows, "comp", axis=0, tiled=True)
     cov_part = inner(reduced_rows, reduced)
-    cov_summed = lax.psum(cov_part, "vox")
+    cov_summed = jnp.sum(lax.all_gather(cov_part, "vox"), axis=0)
     covar = lax.all_gather(cov_summed, "comp", axis=0, tiled=True)
     covar = covar / voxels
     whiten = whitening(covar)

time: 777 us -> 687 us (0.88)
  waiting for transfers between devices: 461 us -> 380 us
  matrix products: 69.2 us -> 58.1 us
  other arithmetic: 7.49 us -> 15.7 us
    psum x1 -> x0, waiting for transfers between devices: 178 us -> none  [shards(): cov_summed = lax.psum(cov_part, 'vox')]
    all_gather x0 -> x1, waiting for transfers between devices: none -> 99.2 us  [shards(): cov_summed = jnp.sum(lax.all_gather(cov_part, 'vox'), axis=0)]
    dot_general x22, matrix products: 57.7 us -> 46.5 us  [mult(): return jnp.dot(left, right, precision=lax.Precision.HIGHEST)]
    reduce_sum x0 -> x1, other arithmetic: none -> 8.23 us  [shards(): cov_summed = jnp.sum(lax.all_gather(cov_part, 'vox'), axis=0)]
where the time goes in v1:
time: 687 us; the launch traced here: 684 us
  waiting for transfers between devices  380 us (55%)
  blocking collectives  211 us (31%)
  matrix products  58.1 us (8%)
  between operations  16.8 us (2%)
  other arithmetic  15.7 us (2%)
    psum x2, blocking collectives, shards(): pulled, slope = lax.psum((pulled, slope), 'vox')  211 us
    psum x2, waiting for transfers between devices, shards(): pulled, slope = lax.psum((pulled, slope), 'vox')  143 us
    all_gather x1, waiting for transfers between devices, shards(): cov_summed = jnp.sum(lax.all_gather(cov_part, 'vox'), axis=0)  99.2 us
    all_gather x2, waiting for transfers between devices, shards(): whole = lax.all_gather(newer, 'comp', axis=0, tiled=True)  51.4 us
    dot_general x22, matrix products, mult(): return jnp.dot(left, right, precision=lax.Precision.HIGHEST)  46.5 us
    reduce_scatter x1, waiting for transfers between devices, shards(): lax.psum_scatter(jnp.dot(projection, data, preferred_element_type=jnp.flo...  35.2 us
    all_gather x1, waiting for transfers between devices, shards(): reduced = lax.all_gather(reduced_rows, 'comp', axis=0, tiled=True)  27 us
    all_gather x1, waiting for transfers between devices, shards(): covar = lax.all_gather(cov_summed, 'comp', axis=0, tiled=True)  24.5 us
  transfers between devices with their start and end apart: 8, of which 8 were waited for; matrix products, arithmetic and copies ran while one was open for 0% of the time, Pallas kernels for 0%

profile of v1, /device:TPU:8, one launch (start us, length us, event | category | flops | bytes accessed | tf_op | source)
XLA Modules:
  0.0 683.9 jit_solution(4541223440491830295)
XLA Ops:
  8.4 3.1 fusion.26
  11.6 35.2 %reduce-scatter.2.cloned.1.call-done = f32[128,1024]{1,0:T(8,128)} async-done(((f32[512,1024]{1,0:T(8,128)}), f32[128,1024]{1,0:T(8,128)}) %reduce-scatter.2.cloned.1.call-update) | async-done | bytes 524304 | tf_op jit(solution)/shard_map/reduce_scatter | solution.py:46
  48.6 27.0 %all-gather.7.cloned.1.call-done = bf16[512,1024]{1,0:T(8,128)(2,1)} async-done(((bf16[128,1024]{1,0:T(8,128)(2,1)}), bf16[512,1024]{1,0:T(8,128)(2,1)}) %all-gather.7.cloned.1.call-update) | async-done | bytes 1048592 | tf_op jit(solution)/shard_map/all_gather | solution.py:52
  75.6 2.5 fusion.27
  78.2 99.2 %all-gather.15.cloned.1.call-done = f32[8192,512]{1,0:T(8,128)} async-done(((f32[128,512]{1,0:T(8,128)}), f32[8192,512]{1,0:T(8,128)}) %all-gather.15.cloned.1.call-update) | async-done | bytes 16777232 | tf_op jit(solution)/shard_map/all_gather | solution.py:54
  177.4 8.2 %reduce_sum.54 = f32[128,512]{1,0:T(8,128)} reduce(f32[64,128,512]{2,1,0:T(8,128)} %bitcast.48, f32[]{:T(128)} %constant.3.clone.1), dimensions={0}, to_apply=%region_1.0 | reduce | flops 4128768 | bytes 17039364 | tf_op jit(solution)/shard_map/reduce_sum | solution.py:54
  186.1 24.5 %all-gather.9.cloned.1.call-done = f32[512,512]{1,0:T(8,128)} async-done(((f32[128,512]{1,0:T(8,128)}), f32[512,512]{1,0:T(8,128)}) %all-gather.9.cloned.1.call-update) | async-done | bytes 1048592 | tf_op jit(solution)/shard_map/all_gather | solution.py:55
  210.7 2.1 multiply_reduce_fusion
  213.5 2.3 select_subtract_fusion.2
  217.0 1.9 fusion.10
  218.9 1.9 select_subtract_fusion.1
  224.5 1.9 select_subtract_fusion
  226.4 2.0 fusion.4
  231.2 105.3 %psum.29 = f32[128]{0:T(128)S(1)} all-reduce(f32[128]{0:T(128)S(1)} %get-tuple-element.2), channel_id=1, replica_groups=mesh['vox'=64,'comp'=4] {'vox'}, use_global_device_ids=true, to_apply=%region_5.0 | all-reduce | flops 128 | bytes 1024 | tf_op jit(solution)/shard_map/psum | solution.py:65
  336.5 71.4 %all-reduce.3.cloned.1.call-done = f32[128,512]{1,0:T(8,128)} async-done(((f32[128,512]{1,0:T(8,128)}), f32[128,512]{1,0:T(8,128)}) %all-reduce.3.cloned.1.call-update) | async-done | bytes 262160 | tf_op jit(solution)/shard_map/psum | solution.py:65
  409.7 25.6 %all-gather.11.cloned.1.call-done = f32[512,512]{1,0:T(8,128)} async-done(((f32[128,512]{1,0:T(8,128)}), f32[512,512]{1,0:T(8,128)}) %all-gather.11.cloned.1.call-update) | async-done | bytes 1048592 | tf_op jit(solution)/shard_map/all_gather | solution.py:67
  435.4 4.2 fusion.6
  440.3 1.9 fusion.8
  442.2 1.9 fusion.3
  444.2 1.9 fusion.30
  446.0 1.9 fusion.2
  447.9 1.9 fusion.31
  449.8 2.8 fusion.32
  455.2 105.5 %psum.31 = f32[128]{0:T(128)S(1)} all-reduce(f32[128]{0:T(128)S(1)} %get-tuple-element.4), channel_id=1, replica_groups=mesh['vox'=64,'comp'=4] {'vox'}, use_global_device_ids=true, to_apply=%region_9.0 | all-reduce | flops 128 | bytes 1024 | tf_op jit(solution)/shard_map/psum | solution.py:65
  560.7 71.2 %all-reduce.5.cloned.1.call-done = f32[128,512]{1,0:T(8,128)} async-done(((f32[128,512]{1,0:T(8,128)}), f32[128,512]{1,0:T(8,128)}) %all-reduce.5.cloned.1.call-update) | async-done | bytes 262160 | tf_op jit(solution)/shard_map/psum | solution.py:65
  633.7 25.7 %all-gather.13.cloned.1.call-done = f32[512,512]{1,0:T(8,128)} async-done(((f32[128,512]{1,0:T(8,128)}), f32[512,512]{1,0:T(8,128)}) %all-gather.13.cloned.1.call-update) | async-done | bytes 1048592 | tf_op jit(solution)/shard_map/all_gather | solution.py:67
  659.5 4.2 fusion.7
  664.4 1.9 fusion.9
  666.4 1.9 fusion.1
  668.3 1.9 fusion.33
  670.1 1.9 fusion
  672.0 1.9 fusion.34
  (44 shorter events, 20.5 us)
Async XLA Ops:
  7.2 1.2 copy-start
  7.2 39.6 %reduce-scatter.2.cloned.1.call-start = ((), (), s32[]{:S(2)}) async-start(), calls=%async_computation.1 | async-start | bytes 2621440 | tf_op jit(solution)/shard_map/reduce_scatter | solution.py:46
  11.5 64.1 %all-gather.7.cloned.1.call-start = ((), (), s32[]{:S(2)}) async-start(), calls=%async_computation.2 | async-start | bytes 1310720 | tf_op jit(solution)/shard_map/all_gather | solution.py:52
  48.6 128.8 %all-gather.15.cloned.1.call-start = ((), (), s32[]{:S(2)}) async-start(), calls=%async_computation.8 | async-start | bytes 17039360 | tf_op jit(solution)/shard_map/all_gather | solution.py:54
  78.1 132.5 %all-gather.9.cloned.1.call-start = ((), (), s32[]{:S(2)}) async-start(), calls=%async_computation.3 | async-start | bytes 1310720 | tf_op jit(solution)/shard_map/all_gather | solution.py:55
  185.6 222.3 %all-reduce.3.cloned.1.call-start = ((), (), s32[]{:S(2)}) async-start(), calls=%async_computation.4 | async-start | bytes 524288 | tf_op jit(solution)/shard_map/psum | solution.py:65
  215.8 1.2 copy-start.4
  226.4 2.1 copy-start.3
  228.5 1.0 copy-start.6
  231.1 204.2 %all-gather.11.cloned.1.call-start = ((), (), s32[]{:S(2)}) async-start(), calls=%async_computation.5 | async-start | bytes 1310720 | tf_op jit(solution)/shard_map/all_gather | solution.py:67
  409.7 222.2 %all-reduce.5.cloned.1.call-start = ((), (), s32[]{:S(2)}) async-start(), calls=%async_computation.6 | async-start | bytes 524288 | tf_op jit(solution)/shard_map/psum | solution.py:65
  435.4 5.0 copy-start.1
  455.2 204.3 %all-gather.13.cloned.1.call-start = ((), (), s32[]{:S(2)}) async-start(), calls=%async_computation.7 | async-start | bytes 1310720 | tf_op jit(solution)/shard_map/all_gather | solution.py:67
  659.5 5.0 copy-start.2
  675.8 1.0 copy-start.5
Sparse Core Ops, SparseCore 0:
  11.6 35.1 reduce-scatter.1
  49.2 26.3 all-gather.6
  79.0 98.3 all-gather.14
  185.7 24.8 all-gather.8
  231.3 176.6 all-reduce.2
  410.2 25.1 all-gather.10
  455.3 176.5 all-reduce.4
  634.3 25.1 all-gather.12
